TPU v7x, 512 devices: a whole 4x8x8 slice. The times are simulated.
512 devices in a mesh: ctx: 32 (over x, z_lo, core), head: 16 (over y, z_hi).
Axes of the slice: x: 4, y: 8, z: 8 (z_hi: 2, z_lo: 4; z = z_hi * 4 + z_lo), core: 2. Of those that a mesh axis runs over, the one named last changes fastest.
Arguments:
- queries: bfloat16 [4096, 8192], P('ctx', 'head'), may hold values from -9 to 9
- keys: bfloat16 [4096, 8192], P('ctx', 'head'), may hold values from -6 to 6
- values: bfloat16 [4096, 8192], P('ctx', 'head'), may hold values from -6 to 6
- d_out: bfloat16 [4096, 8192], P(('ctx', 'head')), may hold values from -6 to 6
- block_lists: int32 [32, 8], replicated, may hold values from 0 to 31, as said below
- list_counts: int32 [32], replicated, may hold values from 1 to 8, as said below
Outputs:
- attn_out: bfloat16 [4096, 8192], P('ctx', 'head')
- grad_q: bfloat16 [4096, 8192], P('ctx', 'head')
- grad_k: bfloat16 [4096, 8192], P('ctx', 'head')
- grad_v: bfloat16 [4096, 8192], P('ctx', 'head')
Inputs may be any that keep to these rules, and one draw needn't show every extreme that they name: `block_lists`: each row holds 8 distinct patch block ids; only the first list_counts entries of a row are read. Patch block p is held by index p of ctx. `list_counts`: some text block reads 8 patch blocks.
All inputs are finite; a program needn't handle non-finite values.
Results may differ from a plain program's by a relative error of at most 0.022.
Values may be sent and summed in bfloat16 or wider, within the bound.
A program may use at most 64 MiB of HBM per device.

v0:
```python
import math
import jax
import jax.numpy as jnp
from jax import lax
from jax.sharding import PartitionSpec as P

DH = 128
BLK = 128


def allowed_table(block_lists, list_counts, total_blocks):
    slot_ids = jnp.arange(block_lists.shape[1], dtype=jnp.int32)
    live_slots = slot_ids[None, :] < list_counts[:, None]
    block_ids = jnp.arange(total_blocks, dtype=jnp.int32)
    matches = (block_lists[:, :, None] == block_ids[None, None, :]) & live_slots[:, :, None]
    return jnp.any(matches, axis=1)


def tile_scores(query_rows, key_rows, scale):
    return (
        jnp.einsum("qhd,khd->hqk", query_rows, key_rows, preferred_element_type=jnp.float32) * scale
    )


def key_tile(heads_array, list_row, slot):
    return lax.dynamic_slice_in_dim(heads_array, list_row[slot] * BLK, BLK, 0)


def listed_forward(q_block, k_heads, v_heads, list_row, list_count, scale):
    heads = q_block.shape[1]

    def first_pass(slot, carry):
        running_max, running_total = carry
        scores = tile_scores(q_block, key_tile(k_heads, list_row, slot), scale)
        new_max = jnp.maximum(running_max, jnp.max(scores, axis=-1))
        running_total = running_total * jnp.exp(running_max - new_max) + jnp.sum(
            jnp.exp(scores - new_max[..., None]), axis=-1
        )
        return (new_max, running_total)

    start_max = jnp.full((heads, BLK), -jnp.inf, jnp.float32)
    start_total = jnp.zeros((heads, BLK), jnp.float32)
    row_max, row_total = lax.fori_loop(0, list_count, first_pass, (start_max, start_total))
    log_total = row_max + jnp.log(row_total)

    def second_pass(slot, acc):
        scores = tile_scores(q_block, key_tile(k_heads, list_row, slot), scale)
        weights = jnp.exp(scores - log_total[..., None]).astype(jnp.bfloat16)
        return acc + jnp.einsum(
            "hqk,khd->qhd",
            weights,
            key_tile(v_heads, list_row, slot),
            preferred_element_type=jnp.float32,
        )

    acc = lax.fori_loop(0, list_count, second_pass, jnp.zeros(q_block.shape, jnp.float32))
    return (log_total, acc.astype(jnp.bfloat16))


def listed_backward(
    q_block, d_block, k_heads, v_heads, list_row, list_count, log_total, row_delta, scale
):

    def tile_pass(slot, acc):
        key_rows = key_tile(k_heads, list_row, slot)
        scores = tile_scores(q_block, key_rows, scale)
        probs = jnp.exp(scores - log_total[..., None])
        dprobs = jnp.einsum(
            "qhd,khd->hqk",
            d_block,
            key_tile(v_heads, list_row, slot),
            preferred_element_type=jnp.float32,
        )
        dscores = (probs * (dprobs - row_delta[..., None])).astype(jnp.bfloat16)
        return acc + jnp.einsum(
            "hqk,khd->qhd", dscores, key_rows, preferred_element_type=jnp.float32
        )

    acc = lax.fori_loop(0, list_count, tile_pass, jnp.zeros(q_block.shape, jnp.float32))
    return (acc * scale).astype(jnp.bfloat16)


def shards(queries, keys, values, d_out, block_lists, list_counts):
    rows = queries.shape[0]
    heads = queries.shape[1] // DH
    scale = 1.0 / math.sqrt(DH)
    local_blocks = rows // BLK
    own_blocks = keys.shape[0] // BLK
    ctx_index = lax.axis_index("ctx")
    k_all, v_all = (
        lax.all_gather(keys, "ctx", axis=0, tiled=True),
        lax.all_gather(values, "ctx", axis=0, tiled=True),
    )
    total_blocks = k_all.shape[0] // BLK
    table = allowed_table(block_lists, list_counts, total_blocks)
    k_heads = k_all.reshape(-1, heads, DH)
    v_heads = v_all.reshape(-1, heads, DH)
    q_heads = queries.reshape(rows, heads, DH)
    d_rows = lax.all_to_all(d_out, "head", split_axis=1, concat_axis=0, tiled=True)
    d_heads = d_rows.reshape(rows, heads, DH)
    block = 0
    global_block = ctx_index * local_blocks + block
    list_row = lax.dynamic_index_in_dim(block_lists, global_block, 0, keepdims=False)
    list_count = lax.dynamic_index_in_dim(list_counts, global_block, 0, keepdims=False)
    log_block, out_block = listed_forward(q_heads, k_heads, v_heads, list_row, list_count, scale)
    delta_rows = jnp.sum(out_block.astype(jnp.float32) * d_heads.astype(jnp.float32), axis=-1).T
    block = 0
    global_block = ctx_index * local_blocks + block
    list_row = lax.dynamic_index_in_dim(block_lists, global_block, 0, keepdims=False)
    list_count = lax.dynamic_index_in_dim(list_counts, global_block, 0, keepdims=False)
    grads_list = listed_backward(
        q_heads, d_heads, k_heads, v_heads, list_row, list_count, log_block, delta_rows, scale
    )
    log_all, delta_all = (
        lax.all_gather(log_block, "ctx", axis=1, tiled=True),
        lax.all_gather(delta_rows, "ctx", axis=1, tiled=True),
    )
    own_table = lax.dynamic_slice_in_dim(table, ctx_index * own_blocks, own_blocks, 1)
    own_keys = jnp.repeat(own_table, BLK, axis=1).astype(jnp.float32)
    text_blocks = own_keys.shape[0]
    k_own = keys.reshape(-1, heads, DH)
    v_own = values.reshape(-1, heads, DH)
    d_piece = lax.all_gather(d_rows, "ctx", axis=0, tiled=True)
    count = d_piece.shape[0]
    row_block = jnp.arange(count, dtype=jnp.int32) // BLK
    one_hot = (row_block[:, None] == jnp.arange(text_blocks, dtype=jnp.int32)[None, :]).astype(
        jnp.float32
    )
    mask = jnp.dot(one_hot, own_keys) > 0.5
    q_three = lax.all_gather(queries, "ctx", axis=0, tiled=True).reshape(count, heads, DH)
    d_three = d_piece.reshape(count, heads, DH)
    scores = tile_scores(q_three, k_own, scale)
    probs = jnp.exp(jnp.where(mask[None], scores - log_all[..., None], -jnp.inf))
    weights = probs.astype(jnp.bfloat16)
    grad_values = jnp.einsum("hqk,qhd->khd", weights, d_three, preferred_element_type=jnp.float32)
    dprobs = jnp.einsum("qhd,khd->hqk", d_three, v_own, preferred_element_type=jnp.float32)
    dscores = (probs * (dprobs - delta_all[..., None])).astype(jnp.bfloat16)
    grad_keys = jnp.einsum("hqk,qhd->khd", dscores, q_three, preferred_element_type=jnp.float32)
    grad_keys, grad_values = (grad_keys, grad_values)
    attn_out = out_block.reshape(rows, heads * DH)
    grad_q = grads_list.reshape(rows, heads * DH)
    grad_k = (grad_keys * scale).astype(jnp.bfloat16).reshape(keys.shape)
    grad_v = grad_values.astype(jnp.bfloat16).reshape(values.shape)
    return (attn_out, grad_q, grad_k, grad_v)


def solution(mesh):
    return jax.shard_map(
        shards,
        mesh=mesh,
        in_specs=(
            P("ctx", "head"),
            P("ctx", "head"),
            P("ctx", "head"),
            P(("ctx", "head"), None),
            P(),
            P(),
        ),
        out_specs=(P("ctx", "head"), P("ctx", "head"), P("ctx", "head"), P("ctx", "head")),
        check_vma=False,
    )
```

profile of v0, /device:TPU:1, one launch (start us, length us, event | category | flops | bytes accessed | tf_op | source)
XLA Modules:
  0.0 357.4 jit_solution(11484293286546743806)
XLA Ops:
  7.2 1.7 copy.110
  8.9 1.7 copy.109
  10.7 1.7 copy.111
  12.4 28.8 %all_to_all.19 = bf16[8,16,512]{2,0,1:T(8,128)(2,1)} all-to-all(bf16[8,16,512]{2,0,1:T(8,128)(2,1)} %bitcast.89), channel_id=1, replica_groups=mesh['ctx'=32,'head'=16] {'head'}, dimensions={1} | all-to-all | bytes 262144 | tf_op jit(solution)/shard_map/all_to_all | solution.py:99
  42.9 1.2 dynamic_slice.41
  47.2 44.3 %all-gather.7.cloned.1.call-done = bf16[4096,512]{0,1:T(8,128)(2,1)} async-done(((bf16[128,512]{0,1:T(8,128)(2,1)}), bf16[4096,512]{0,1:T(8,128)(2,1)}) %all-gather.7.cloned.1.call-update) | async-done | bytes 4194320 | tf_op jit(solution)/shard_map/all_gather | solution.py:91
  91.5 6.3 %copy.114 = bf16[4096,4,128]{2,0,1:T(8,128)(2,1)} copy(bf16[4096,4,128]{0,2,1:T(8,128)(2,1)} %bitcast.76) | data formatting | bytes 8388608 | tf_op jit(solution)/shard_map/while | solution.py:56
  97.9 12.8 %while.32 = (s32[]{:T(128)}, f32[4,128]{1,0:T(4,128)S(1)}, f32[4,128]{1,0:T(4,128)S(1)}, s32[]{:T(128)}, s32[8]{0:T(128)S(1)}, /*index=5*/bf16[4096,4,128]{2,0,1...) while((s32[]{:T(128)}, f32[4,128]{1,0:T(4,128)S(1)}, ...), condition=%wide.region_3.4_spmd, body=%wide.region_0.3_spmd.sunk | while | flops 17040392 | bytes 813277 | solution.py:43
  99.7 1.1 fusion.74
  102.8 1.1 fusion.74
  105.8 1.1 fusion.74
  108.9 1.1 fusion.74
  110.7 57.2 %all-gather.5.cloned.1.call-done = bf16[4096,512]{0,1:T(8,128)(2,1)} async-done(((bf16[128,512]{0,1:T(8,128)(2,1)}), bf16[4096,512]{0,1:T(8,128)(2,1)}) %all-gather.5.cloned.1.call-update) | async-done | bytes 4194320 | tf_op jit(solution)/shard_map/all_gather | solution.py:92
  167.9 13.3 %while.33 = (s32[]{:T(128)}, f32[128,4,128]{0,2,1:T(8,128)S(1)}, s32[]{:T(128)}, s32[8]{0:T(128)S(1)}, bf16[4096,4,128]{0,2,1:T(8,128)(2,1)}, /*index=5*/bf16[40...) while((s32[]{:T(128)}, f32[128,4,128]{0,2,1:T(8,128)S(1)}, ...), condition=%wide.region_5.6_spmd, body=%wide.region_4.5_spmd.sunk | while | flops 33816584 | bytes 920801 | solution.py:56
  169.7 1.4 fusion.78
  172.9 1.3 fusion.78
  176.1 1.4 fusion.78
  179.3 1.3 fusion.78
  182.3 18.1 %while.34 = (s32[]{:T(128)}, f32[128,4,128]{0,2,1:T(8,128)S(1)}, s32[]{:T(128)}, s32[8]{0:T(128)S(1)}, bf16[4096,4,128]{2,0,1:T(8,128)(2,1)}, /*index=5*/bf16[12...) while((s32[]{:T(128)}, f32[128,4,128]{0,2,1:T(8,128)S(1)}, ...), condition=%wide.region_8.9_spmd, body=%wide.region_7.8_spmd.sunk | while | flops 50724872 | bytes 1709301 | solution.py:79
  184.1 1.1 fusion.84
  185.3 1.4 fusion.85
  188.5 1.1 fusion.84
  189.6 1.4 fusion.85
  192.9 1.1 fusion.84
  194.0 1.4 fusion.85
  198.4 1.4 fusion.85
  201.2 79.8 %all_gather.23 = f32[4,4096]{0,1:T(8,128)S(1)} all-gather(f32[4,128]{0,1:T(8,128)S(1)} %bitcast.83), channel_id=1, replica_groups=mesh['ctx'=32,'head'=16] {'ctx'}, dimensions={1}, use_global_device_ids=true | all-gather | bytes 67584 | tf_op jit(solution)/shard_map/all_gather | solution.py:116
  281.6 39.7 %all_gather.21 = f32[4,4096]{1,0:T(4,128)S(1)} all-gather(f32[4,128]{1,0:T(4,128)S(1)} %get-tuple-element.646), channel_id=1, replica_groups=mesh['ctx'=32,'head'=16] {'ctx'}, dimensions={1}, use_global_device_ids=true | all-gather | bytes 67584 | tf_op jit(solution)/shard_map/all_gather | solution.py:115
  321.3 7.8 %select_exponential_fusion = f32[4,4096,128]{2,1,0:T(8,128)} fusion(bf16[4096,4,128]{0,2,1:T(8,128)(2,1)} %bitcast.77, f32[4,4096]{1,0:T(4,128)S(1)} %all_gather.21, pred[4096,128]{1,0:T(8,128)(4,1)S(1)} %convolution_compare_fusion, bf16[128,512]{1,0:T(8,128)(2,1)S(1)} %copy-done.2), kind=kOutput, calls=%fused_computation.33 | convolution fusion | flops 543162368 | bytes 13303808 | tf_op jit(solution)/shard_map/qhd,khd->hqk/dot_general | solution.py:21
  329.1 6.5 %copy.129 = bf16[4096,512]{0,1:T(8,128)(2,1)} copy(bf16[4096,512]{1,0:T(8,128)(2,1)} %all-gather.11.cloned.1.call-done) | data formatting | bytes 8388608 | tf_op jit(solution)/shard_map/all_gather | solution.py:123
  335.5 5.9 %fusion.33 = bf16[4,128,128]{1,2,0:T(8,128)(2,1)S(1)} fusion(bf16[4096,4,128]{0,2,1:T(8,128)(2,1)} %bitcast.74, f32[4,4096,128]{2,1,0:T(8,128)} %select_exponential_fusion), kind=kOutput, calls=%fused_computation.40 | convolution fusion | flops 539033600 | bytes 12713984 | tf_op jit(solution)/shard_map/hqk,qhd->khd/dot_general | solution.py:135
  341.5 7.9 %fusion.32 = bf16[4,128,128]{1,2,0:T(8,128)(2,1)S(1)} fusion(bf16[4096,4,128]{0,2,1:T(8,128)(2,1)} %bitcast.78, f32[4,4096,128]{2,1,0:T(8,128)} %select_exponential_fusion, bf16[4096,4,128]{0,2,1:T(8,128)(2,1)} %bitcast.75, f32[4,4096]{1,0:T(4,128)S(1)} %copy.132, bf16[128,512]{1,0:T(8,128)(2,1)S(1)} %copy-done.1), kind=kOutput, calls=%fused_computation.39 | convolution fusion | flops 1080164352 | bytes 17104896 | tf_op jit(solution)/shard_map/hqk,qhd->khd/dot_general | solution.py:138
  (70 shorter events, 17.5 us)
Async XLA Ops:
  7.2 84.3 %all-gather.7.cloned.1.call-start = ((), (), s32[]{:S(2)}) async-start(), calls=%async_computation.2 | async-start | bytes 4325376 | tf_op jit(solution)/shard_map/all_gather | solution.py:91
  8.9 159.0 %all-gather.5.cloned.1.call-start = ((), (), s32[]{:S(2)}) async-start(), calls=%async_computation.1 | async-start | bytes 4325376 | tf_op jit(solution)/shard_map/all_gather | solution.py:92
  10.6 310.6 %all-gather.9.cloned.1.call-start = ((), (), s32[]{:S(2)}) async-start(), calls=%async_computation.3 | async-start | bytes 4325376 | tf_op jit(solution)/shard_map/all_gather | solution.py:130
  12.4 316.7 %all-gather.11.cloned.1.call-start = ((), (), s32[]{:S(2)}) async-start(), calls=%async_computation.4 | async-start | bytes 4325376 | tf_op jit(solution)/shard_map/all_gather | solution.py:123
  41.2 5.8 %copy-start = (bf16[8,16,512]{2,0,1:T(8,128)(2,1)S(1)}, bf16[8,16,512]{2,0,1:T(8,128)(2,1)}, u32[]{:S(2)}) copy-start(bf16[8,16,512]{2,0,1:T(8,128)(2,1)} %all_to_all.19) | copy-start | bytes 393220
  200.3 120.9 %copy-start.2 = (bf16[128,512]{1,0:T(8,128)(2,1)S(1)}, bf16[128,512]{1,0:T(8,128)(2,1)}, u32[]{:S(2)}) copy-start(bf16[128,512]{1,0:T(8,128)(2,1)} %param.13) | copy-start | bytes 393220
  335.5 5.9 %copy-start.1 = (bf16[128,512]{1,0:T(8,128)(2,1)S(1)}, bf16[128,512]{1,0:T(8,128)(2,1)}, u32[]{:S(2)}) copy-start(bf16[128,512]{1,0:T(8,128)(2,1)} %param.14) | copy-start | bytes 393220
Sparse Core Ops, SparseCore 0:
  10.6 80.8 all-gather.6
  94.1 73.7 all-gather.4
  170.5 74.7 all-gather.8
  247.3 66.9 all-gather.10
where the time goes:
time: 359 us; the launch traced here: 357 us
  blocking collectives  148 us (41%)
  waiting for transfers between devices  102 us (28%)
  matrix products  42.4 us (12%)
  local copies, waits for them, and re-layouts  33.1 us (9%)
  loops' own time  16.8 us (5%)
  between operations  13.9 us (4%)
    all_gather x1, blocking collectives, shards(): lax.all_gather(delta_rows, 'ctx', axis=1, tiled=True)  79.8 us
    all_gather x1, waiting for transfers between devices, shards(): lax.all_gather(values, 'ctx', axis=0, tiled=True)  57.2 us
    all_gather x1, waiting for transfers between devices, shards(): lax.all_gather(keys, 'ctx', axis=0, tiled=True)  44.3 us
    all_gather x1, blocking collectives, shards(): lax.all_gather(log_block, 'ctx', axis=1, tiled=True)  39.7 us
    all_to_all x1, blocking collectives, shards(): lax.all_to_all(d_out, 'head', split_axis=1, concat_axis=0, tiled=True)  28.8 us
    dot_general x9, matrix products, tile_scores(): jnp.einsum('qhd,khd->hqk', query_rows, key_rows, preferred_element_type=j...  16.9 us
    dot_general x1, matrix products, shards(): jnp.einsum('hqk,qhd->khd', dscores, q_three, preferred_element_type=jnp.f...  7.87 us
    unnamed x13, local copies, waits for them, and re-layouts  7.46 us
  transfers between devices with their start and end apart: 4, of which 2 were waited for; matrix products, arithmetic and copies ran while one was open for 15% of the time, Pallas kernels for 0%

commit v1 on v0

--- a/solution.py
+++ b/solution.py
@@ -1,11 +1,22 @@
+import functools
 import math
 import jax
 import jax.numpy as jnp
 from jax import lax
 from jax.sharding import PartitionSpec as P
+from jax.lax import all_to_all, axis_size
 
 DH = 128
 BLK = 128
+
+
+def _fit_marks(x_in, shard_axis):
+    taken_in = jnp.stack([x_in for _ in range(axis_size(shard_axis))])
+    outcome_arr = all_to_all(taken_in, shard_axis, concat_axis=0, split_axis=0)
+    return jnp.concatenate(outcome_arr, axis=1)
+
+
+recover_lane = functools.partial(_fit_marks, shard_axis="ctx")
 
 
 def allowed_table(block_lists, list_counts, total_blocks):
@@ -112,7 +123,7 @@
         q_heads, d_heads, k_heads, v_heads, list_row, list_count, log_block, delta_rows, scale
     )
     log_all, delta_all = (
-        lax.all_gather(log_block, "ctx", axis=1, tiled=True),
+        recover_lane(log_block),
         lax.all_gather(delta_rows, "ctx", axis=1, tiled=True),
     )
     own_table = lax.dynamic_slice_in_dim(table, ctx_index * own_blocks, own_blocks, 1)

time: 359 us -> 346 us (0.964)
  blocking collectives: 148 us -> 111 us
  starting transfers between devices: 0.16 us -> 16.5 us
  waiting for transfers between devices: 102 us -> 107 us
    all_gather x1 -> x0, blocking collectives: 39.7 us -> none  [shards(): lax.all_gather(log_block, 'ctx', axis=1, tiled=True)]
    all_gather x1, waiting for transfers between devices: 0.01 us -> 21.5 us  [shards(): d_piece = lax.all_gather(d_rows, 'ctx', axis=0, tiled=True)]
    all_to_all x0 -> x1, starting transfers between devices: none -> 16.4 us  [_fit_marks(): outcome_arr = all_to_all(taken_in, shard_axis, concat_axis=0, split_axis=0)]
    all_gather x1, waiting for transfers between devices: 57.2 us -> 41.2 us  [shards(): lax.all_gather(values, 'ctx', axis=0, tiled=True)]
  transfers between devices with their start and end apart: 4 -> 5, of which waited for: 2 -> 3; matrix products, arithmetic and copies ran while one was open for 15% -> 16% of each run, Pallas kernels for 0% -> 0%
where the time goes in v1:
time: 346 us; the launch traced here: 344 us
  blocking collectives  111 us (32%)
  waiting for transfers between devices  107 us (31%)
  matrix products  42.5 us (12%)
  local copies, waits for them, and re-layouts  33.8 us (10%)
  loops' own time  18.3 us (5%)
  starting transfers between devices  16.5 us (5%)
  between operations  13.9 us (4%)
    all_gather x1, blocking collectives, shards(): lax.all_gather(delta_rows, 'ctx', axis=1, tiled=True)  82.3 us
    all_gather x1, waiting for transfers between devices, shards(): lax.all_gather(keys, 'ctx', axis=0, tiled=True)  44.2 us
    all_gather x1, waiting for transfers between devices, shards(): lax.all_gather(values, 'ctx', axis=0, tiled=True)  41.2 us
    all_to_all x1, blocking collectives, shards(): lax.all_to_all(d_out, 'head', split_axis=1, concat_axis=0, tiled=True)  28.8 us
    all_gather x1, waiting for transfers between devices, shards(): d_piece = lax.all_gather(d_rows, 'ctx', axis=0, tiled=True)  21.5 us
    dot_general x9, matrix products, tile_scores(): jnp.einsum('qhd,khd->hqk', query_rows, key_rows, preferred_element_type=j...  17 us
    all_to_all x1, starting transfers between devices, _fit_marks(): outcome_arr = all_to_all(taken_in, shard_axis, concat_axis=0, split_axis=0)  16.4 us
    dot_general x1, matrix products, shards(): jnp.einsum('hqk,qhd->khd', dscores, q_three, preferred_element_type=jnp.f...  7.87 us
  transfers between devices with their start and end apart: 5, of which 3 were waited for; matrix products, arithmetic and copies ran while one was open for 16% of the time, Pallas kernels for 0%

profile of v1, /device:TPU:1, one launch (start us, length us, event | category | flops | bytes accessed | tf_op | source)
XLA Modules:
  0.0 344.4 jit_solution(12786631848269061400)
XLA Ops:
  7.2 1.7 copy.110
  8.9 1.7 copy.109
  10.7 1.7 copy.111
  12.4 28.8 %all_to_all.24 = bf16[8,16,512]{2,0,1:T(8,128)(2,1)} all-to-all(bf16[8,16,512]{2,0,1:T(8,128)(2,1)} %bitcast.92), channel_id=1, replica_groups=mesh['ctx'=32,'head'=16] {'head'}, dimensions={1} | all-to-all | bytes 262144 | tf_op jit(solution)/shard_map/all_to_all | solution.py:110
  42.9 1.3 dynamic_slice.41
  47.3 44.2 %all-gather.7.cloned.1.call-done = bf16[4096,512]{0,1:T(8,128)(2,1)} async-done(((bf16[128,512]{0,1:T(8,128)(2,1)}), bf16[4096,512]{0,1:T(8,128)(2,1)}) %all-gather.7.cloned.1.call-update) | async-done | bytes 4194320 | tf_op jit(solution)/shard_map/all_gather | solution.py:102
  91.5 6.4 %copy.114 = bf16[4096,4,128]{2,0,1:T(8,128)(2,1)} copy(bf16[4096,4,128]{0,2,1:T(8,128)(2,1)} %bitcast.79) | data formatting | bytes 8388608 | tf_op jit(solution)/shard_map/while | solution.py:67
  97.9 13.3 %while.32 = (s32[]{:T(128)}, f32[4,128]{1,0:T(4,128)S(1)}, f32[4,128]{1,0:T(4,128)S(1)}, s32[]{:T(128)}, s32[8]{0:T(128)S(1)}, /*index=5*/bf16[4096,4,128]{2,0,1...) while((s32[]{:T(128)}, f32[4,128]{1,0:T(4,128)S(1)}, ...), condition=%wide.region_3.4_spmd, body=%wide.region_0.3_spmd.sunk | while | flops 17040392 | bytes 813277 | solution.py:54
  99.8 1.1 fusion.74
  103.0 1.1 fusion.74
  106.1 1.1 fusion.74
  109.3 1.1 fusion.74
  111.9 16.4 %all-to-all-start.1 = ((f32[32,4,128]{2,1,0:T(4,128)}), f32[32,4,128]{2,1,0:T(4,128)S(1)}, u32[]{:S(2)}, u32[]{:S(2)}) async-start(f32[32,4,128]{2,1,0:T(4,128)} %stack.2), calls=%async_computation.1 | async-start | bytes 131072 | tf_op jit(solution)/shard_map/all_to_all | solution.py:15
  128.2 41.2 %all-gather.5.cloned.1.call-done = bf16[4096,512]{0,1:T(8,128)(2,1)} async-done(((bf16[128,512]{0,1:T(8,128)(2,1)}), bf16[4096,512]{0,1:T(8,128)(2,1)}) %all-gather.5.cloned.1.call-update) | async-done | bytes 4194320 | tf_op jit(solution)/shard_map/all_gather | solution.py:103
  169.5 13.8 %while.33 = (s32[]{:T(128)}, f32[128,4,128]{0,2,1:T(8,128)S(1)}, s32[]{:T(128)}, s32[8]{0:T(128)S(1)}, bf16[4096,4,128]{0,2,1:T(8,128)(2,1)}, /*index=5*/bf16[40...) while((s32[]{:T(128)}, f32[128,4,128]{0,2,1:T(8,128)S(1)}, ...), condition=%wide.region_5.6_spmd, body=%wide.region_4.5_spmd.sunk | while | flops 33816584 | bytes 920801 | solution.py:67
  171.4 1.4 fusion.78
  174.7 1.3 fusion.78
  178.0 1.4 fusion.78
  181.3 1.3 fusion.78
  183.6 18.6 %while.34 = (s32[]{:T(128)}, f32[128,4,128]{0,2,1:T(8,128)S(1)}, s32[]{:T(128)}, s32[8]{0:T(128)S(1)}, bf16[4096,4,128]{2,0,1:T(8,128)(2,1)}, /*index=5*/bf16[12...) while((s32[]{:T(128)}, f32[128,4,128]{0,2,1:T(8,128)S(1)}, ...), condition=%wide.region_8.9_spmd, body=%wide.region_7.8_spmd.sunk | while | flops 50724872 | bytes 1709301 | solution.py:90
  186.6 1.4 fusion.85
  191.1 1.4 fusion.85
  194.4 1.1 fusion.84
  195.6 1.4 fusion.85
  198.9 1.1 fusion.84
  200.1 1.4 fusion.85
  203.7 82.3 %all_gather.19 = f32[4,4096]{0,1:T(8,128)S(1)} all-gather(f32[4,128]{0,1:T(8,128)S(1)} %bitcast.86), channel_id=1, replica_groups=mesh['ctx'=32,'head'=16] {'ctx'}, dimensions={1}, use_global_device_ids=true | all-gather | bytes 67584 | tf_op jit(solution)/shard_map/all_gather | solution.py:127
  286.7 7.9 %select_exponential_fusion = f32[4,4096,128]{2,1,0:T(8,128)} fusion(bf16[4096,4,128]{0,2,1:T(8,128)(2,1)} %bitcast.80, f32[4,4096]{1,0:T(4,128)S(1)} %bitcast.93, pred[4096,128]{1,0:T(8,128)(4,1)S(1)} %convolution_compare_fusion, bf16[128,512]{1,0:T(8,128)(2,1)S(1)} %copy-done.2), kind=kOutput, calls=%fused_computation.33 | convolution fusion | flops 543162368 | bytes 13303808 | tf_op jit(solution)/shard_map/qhd,khd->hqk/dot_general | solution.py:32
  294.6 21.5 %all-gather.11.cloned.1.call-done = bf16[4096,512]{1,0:T(8,128)(2,1)} async-done(((bf16[128,512]{1,0:T(8,128)(2,1)}), bf16[4096,512]{1,0:T(8,128)(2,1)}) %all-gather.11.cloned.1.call-update) | async-done | bytes 4194320 | tf_op jit(solution)/shard_map/all_gather | solution.py:134
  316.1 6.4 %copy.129 = bf16[4096,512]{0,1:T(8,128)(2,1)} copy(bf16[4096,512]{1,0:T(8,128)(2,1)} %all-gather.11.cloned.1.call-done) | data formatting | bytes 8388608 | tf_op jit(solution)/shard_map/all_gather | solution.py:134
  322.5 5.9 %fusion.33 = bf16[4,128,128]{1,2,0:T(8,128)(2,1)S(1)} fusion(bf16[4096,4,128]{0,2,1:T(8,128)(2,1)} %bitcast.77, f32[4,4096,128]{2,1,0:T(8,128)} %select_exponential_fusion), kind=kOutput, calls=%fused_computation.40 | convolution fusion | flops 539033600 | bytes 12713984 | tf_op jit(solution)/shard_map/hqk,qhd->khd/dot_general | solution.py:146
  328.4 7.9 %fusion.32 = bf16[4,128,128]{1,2,0:T(8,128)(2,1)S(1)} fusion(bf16[4096,4,128]{0,2,1:T(8,128)(2,1)} %bitcast.81, f32[4,4096,128]{2,1,0:T(8,128)} %select_exponential_fusion, bf16[4096,4,128]{0,2,1:T(8,128)(2,1)} %bitcast.78, f32[4,4096]{1,0:T(4,128)S(1)} %copy.132, bf16[128,512]{1,0:T(8,128)(2,1)S(1)} %copy-done.1), kind=kOutput, calls=%fused_computation.39 | convolution fusion | flops 1080164352 | bytes 17104896 | tf_op jit(solution)/shard_map/hqk,qhd->khd/dot_general | solution.py:149
  (72 shorter events, 19.3 us)
Async XLA Ops:
  7.2 84.4 %all-gather.7.cloned.1.call-start = ((), (), s32[]{:S(2)}) async-start(), calls=%async_computation.3 | async-start | bytes 4325376 | tf_op jit(solution)/shard_map/all_gather | solution.py:102
  8.9 160.5 %all-gather.5.cloned.1.call-start = ((), (), s32[]{:S(2)}) async-start(), calls=%async_computation.2 | async-start | bytes 4325376 | tf_op jit(solution)/shard_map/all_gather | solution.py:103
  10.6 276.0 %all-gather.9.cloned.1.call-start = ((), (), s32[]{:S(2)}) async-start(), calls=%async_computation.4 | async-start | bytes 4325376 | tf_op jit(solution)/shard_map/all_gather | solution.py:141
  12.4 303.7 %all-gather.11.cloned.1.call-start = ((), (), s32[]{:S(2)}) async-start(), calls=%async_computation.5 | async-start | bytes 4325376 | tf_op jit(solution)/shard_map/all_gather | solution.py:134
  41.2 5.9 %copy-start = (bf16[8,16,512]{2,0,1:T(8,128)(2,1)S(1)}, bf16[8,16,512]{2,0,1:T(8,128)(2,1)}, u32[]{:S(2)}) copy-start(bf16[8,16,512]{2,0,1:T(8,128)(2,1)} %all_to_all.24) | copy-start | bytes 393220
  111.9 174.8 %all-to-all-start.1 = ((f32[32,4,128]{2,1,0:T(4,128)}), f32[32,4,128]{2,1,0:T(4,128)S(1)}, u32[]{:S(2)}, u32[]{:S(2)}) async-start(f32[32,4,128]{2,1,0:T(4,128)} %stack.2), calls=%async_computation.1 | async-start | bytes 131072 | tf_op jit(solution)/shard_map/all_to_all | solution.py:15
  202.1 84.5 %copy-start.2 = (bf16[128,512]{1,0:T(8,128)(2,1)S(1)}, bf16[128,512]{1,0:T(8,128)(2,1)}, u32[]{:S(2)}) copy-start(bf16[128,512]{1,0:T(8,128)(2,1)} %param.13) | copy-start | bytes 393220
  322.5 5.9 %copy-start.1 = (bf16[128,512]{1,0:T(8,128)(2,1)S(1)}, bf16[128,512]{1,0:T(8,128)(2,1)}, u32[]{:S(2)}) copy-start(bf16[128,512]{1,0:T(8,128)(2,1)} %param.14) | copy-start | bytes 393220
Sparse Core Ops, SparseCore 0:
  10.6 80.8 all-gather.6
  94.1 75.2 all-gather.4
  172.1 73.1 all-gather.8
  247.3 68.7 all-gather.10
